TPU v7x, 128 devices: a whole 4x4x4 slice. The times are simulated.
128 devices in a mesh: grid: 32 (over z, x, core), rep: 4 (over y).
Axes of the slice: x: 4, y: 4, z: 4, core: 2. Of those that a mesh axis runs over, the one named last changes fastest.
Arguments:
- functions: bfloat16 [8192, 32768], P(('grid', 'rep')), may hold values from -6 to 6
- filter_taps: bfloat16 [16], replicated, may hold values from -0.59765625 to 0.59765625
- potential: float32 [32768], replicated, may hold values from 0 to 1
- energies: float32 [8192], P(('grid', 'rep')), may hold values from -1.5 to -0.5
- region_start: int32 [8192], P(('grid', 'rep')), may hold values from 0 to 128
- region_length: int32 [8192], P(('grid', 'rep')), may hold values from 256 to 384
- partner_groups: int32 [128, 3], replicated, may hold values from 0 to 127, as said below
Outputs:
- corrected: bfloat16 [8192, 32768], P(('grid', 'rep'))
Inputs may be any that keep to these rules, and one draw needn't show every extreme that they name: `partner_groups`: the 3 entries of a row are distinct and differ from the row's own group; each is the row's group plus an offset of magnitude 1 to 63, modulo 128.
All inputs are finite; a program needn't handle non-finite values.
Results may differ from a plain program's by a relative error of at most 0.005.
Values may be sent and summed in bfloat16 or wider, within the bound.
A program may use at most 128 MiB of HBM per device.

v0:
```python
import jax
import jax.numpy as jnp
from jax import lax
from jax.sharding import PartitionSpec as P

SIDE = 32
NC = 32768
BLOCK = 64
GROUP = 64
TAPS = 16
PARTNERS = 3
LMAX = 384


def filter_matrix(filter_taps, extent):
    centre = TAPS // 2
    inputs = jnp.arange(extent, dtype=jnp.int32)
    distance = inputs[:, None] - inputs[None, :] + centre
    choose = (distance[:, :, None] == jnp.arange(TAPS, dtype=jnp.int32)[None, None, :]).astype(
        jnp.float32
    )
    return jnp.sum(choose * filter_taps.astype(jnp.float32)[None, None, :], axis=2)


def on_device(
    functions, filter_taps, potential, energies, region_start, region_length, partner_groups
):
    count_rows = functions.shape[0]
    grid_size = lax.axis_size("grid")
    rep_size = lax.axis_size("rep")
    devices_all = grid_size * rep_size
    local_cols = NC // devices_all
    single = filter_matrix(filter_taps, SIDE)
    ident = jnp.eye(SIDE, dtype=jnp.float32)
    plane_matrix = (jnp.kron(single, ident) + jnp.kron(ident, single)).astype(jnp.bfloat16)
    line_matrix = single.astype(jnp.bfloat16)
    slabs = functions.reshape(count_rows, SIDE, SIDE * SIDE)
    plane_part = jnp.dot(
        functions.reshape(count_rows * SIDE, SIDE * SIDE),
        plane_matrix,
        preferred_element_type=jnp.float32,
    ).reshape(count_rows, SIDE, SIDE * SIDE)
    line_part = jnp.einsum("fxc,xw->fwc", slabs, line_matrix, preferred_element_type=jnp.float32)
    kinetic = (plane_part + line_part).reshape(count_rows, NC)
    values = functions.astype(jnp.float32)
    gradient = kinetic + potential[None, :] * values - energies[:, None] * values
    updated = values - 0.3 * gradient / (1.0 - energies)[:, None]
    block_index = jnp.arange(NC, dtype=jnp.int32) // BLOCK
    inside = (block_index[None, :] >= region_start[:, None]) & (
        block_index[None, :] < (region_start + region_length)[:, None]
    )
    refined = jnp.where(inside, updated, 0.0).astype(jnp.bfloat16)
    gridded = lax.all_to_all(refined, ("grid", "rep"), split_axis=1, concat_axis=0, tiled=True)
    group_count = gridded.shape[0] // GROUP
    grouped = gridded.reshape(group_count, GROUP, local_cols)
    partner_rows = grouped[partner_groups]
    stacked = jnp.concatenate([grouped[:, None], partner_rows], axis=1)
    local_intersection = jnp.einsum(
        "agc,akhc->akgh", grouped, stacked, preferred_element_type=jnp.float32
    )
    weight = 1.0 / (BLOCK * LMAX)
    identity_block = jnp.concatenate(
        [jnp.eye(GROUP, dtype=jnp.float32)[None], jnp.zeros((PARTNERS, GROUP, GROUP), jnp.float32)],
        axis=0,
    )
    summed = lax.psum(local_intersection, ("grid", "rep"))
    coupling = (0.5 * (summed * weight - identity_block[None])).astype(jnp.bfloat16)
    shifted = jnp.einsum("akgh,akhc->agc", coupling, stacked, preferred_element_type=jnp.float32)
    result_grid = (grouped.astype(jnp.float32) - shifted).astype(jnp.bfloat16)
    result_grid = result_grid.reshape(group_count * GROUP, local_cols)
    return lax.all_to_all(result_grid, ("grid", "rep"), split_axis=0, concat_axis=1, tiled=True)


def solution(mesh):
    return jax.shard_map(
        on_device,
        mesh=mesh,
        in_specs=(
            P(("grid", "rep"), None),
            P(),
            P(),
            P(("grid", "rep")),
            P(("grid", "rep")),
            P(("grid", "rep")),
            P(),
        ),
        out_specs=P(("grid", "rep"), None),
        check_vma=False,
    )
```

profile of v0, /device:TPU:1, one launch (start us, length us, event | category | flops | bytes accessed | tf_op | source)
XLA Modules:
  0.0 433.5 jit_solution(11363357073585440919)
XLA Ops:
  6.6 0.7 convert_element_type.56
  7.2 0.1 select_reduce_fusion
  7.4 5.9 %add_convert_fusion = bf16[32,32,32,32]{3,2,1,0:T(8,128)(2,1)} fusion(f32[32,32]{1,0:T(8,128)S(1)} %select_reduce_fusion, f32[32,32]{1,0:T(8,128)S(1)} %fusion.13), kind=kLoop, calls=%fused_computation.2 | loop fusion | flops 4194304 | bytes 2105344 | tf_op jit(solution)/shard_map/convert_element_type | solution.py:35
  13.3 11.3 %convert_element_type.59 = bf16[1024,1024]{1,0:T(8,128)(2,1)S(1)} reshape(bf16[32,32,32,32]{3,2,1,0:T(8,128)(2,1)} %add_convert_fusion) | data formatting | bytes 4194304 | tf_op jit(solution)/shard_map/convert_element_type | solution.py:35
  24.6 7.4 %reshape.111 = bf16[2048,1024]{1,0:T(8,128)(2,1)} reshape(bf16[64,32768]{1,0:T(8,128)(2,1)} %param.7) | data formatting | bytes 8388608 | tf_op jit(solution)/shard_map/reshape | solution.py:39
  32.0 9.0 %convolution_bitcast_fusion = f32[2048,1024]{0,1:T(8,128)} fusion(bf16[1024,1024]{1,0:T(8,128)(2,1)S(1)} %convert_element_type.59, bf16[2048,1024]{1,0:T(8,128)(2,1)} %reshape.111), kind=kOutput, calls=%fused_computation.18 | convolution fusion | flops 4294967296 | bytes 14680064 | tf_op jit(solution)/shard_map/dot_general | solution.py:38
  41.0 9.2 %copy.24 = f32[2048,1024]{1,0:T(8,128)} copy(f32[2048,1024]{0,1:T(8,128)} %convolution_bitcast_fusion) | data formatting | bytes 16777216 | tf_op jit(solution)/shard_map/dot_general | solution.py:38
  50.2 0.0 copy-start.1
  50.2 4.8 %copy.38 = bf16[8,8,32,1024]{3,2,1,0:T(8,128)(2,1)S(1)} copy(bf16[8,8,32,1024]{3,1,2,0:T(8,128)(2,1)} %bitcast.44) | data formatting | bytes 8388608
  55.0 0.0 copy-done.1
  55.0 1.3 bitcast_add_fusion
  56.3 0.0 copy-start.4
  56.3 0.0 copy-start.5
  56.3 0.0 copy-start.6
  56.3 0.0 copy-start
  56.4 0.0 copy-start.2
  56.4 5.0 %copy.39 = f32[8,8,32,1024]{3,1,2,0:T(8,128)S(1)} copy(f32[8,8,32,1024]{3,2,1,0:T(8,128)S(1)} %bitcast.48) | data formatting | bytes 16777216
  61.4 0.0 copy-done.4
  61.4 0.0 copy-done.5
  61.5 0.0 copy-done.6
  61.5 0.0 copy-done
  61.5 0.0 copy-done.2
  61.5 3.5 fusion.8
  65.0 0.0 copy-start.3
  65.1 2.6 copy.41
  67.6 11.9 %all-to-all-start = ((bf16[64,128,256]{2,0,1:T(8,128)(2,1)}), bf16[64,128,256]{2,0,1:T(8,128)(2,1)}, u32[]{:S(2)}, u32[]{:S(2)}) async-start(bf16[64,128,256]{2,0,1:T(8,128)(2,1)} %bitcast.50), calls=%async_computation | async-start | bytes 8388608 | tf_op jit(solution)/shard_map/all_to_all | solution.py:53
  79.6 0.3 all-reduce.3.cloned.1.call-start
  79.9 0.0 copy-done.3
  79.9 0.1 copy.27
  80.0 0.2 reshape.117
  80.2 52.2 %all-to-all-done = bf16[64,128,256]{2,0,1:T(8,128)(2,1)} async-done(((bf16[64,128,256]{2,0,1:T(8,128)(2,1)}), bf16[64,128,256]{2,0,1:T(8,128)(2,1)}, u32[]{:S(2)}, u32[]{:S(2)}) %all-to-all-start) | async-done | bytes 4194336 | tf_op jit(solution)/shard_map/all_to_all | solution.py:53
  132.4 13.5 %gather_fusion = bf16[384,64,256]{2,1,0:T(8,128)(2,1)} fusion(bf16[128,64,256]{2,1,0:T(8,128)(2,1)} %bitcast.4, s32[1024]{0:T(1024)S(1)} %pad_clamp_fusion), kind=kCustom, calls=%fused_computation | custom fusion | bytes 25167360 | tf_op jit(solution)/shard_map/gather | solution.py:56
  145.9 12.7 %fusion.1 = f32[128,4,64,64]{3,2,1,0:T(8,128)} fusion(bf16[128,3,64,256]{3,2,1,0:T(8,128)(2,1)} %bitcast.53, bf16[128,1,64,256]{3,2,1,0:T(8,128)(2,1)} %bitcast.6, bf16[64,128,256]{2,0,1:T(8,128)(2,1)} %all-to-all-done), kind=kOutput, calls=%fused_computation.7 | convolution fusion | flops 1082130432 | bytes 29360128 | tf_op jit(solution)/shard_map/agc,akhc->akgh/dot_general | solution.py:58
  158.6 15.7 %copy.29 = f32[128,4,64,64]{0,2,3,1:T(8,128)} copy(f32[128,4,64,64]{3,2,1,0:T(8,128)} %fusion.1) | data formatting | bytes 16777216 | tf_op jit(solution)/shard_map/agc,akhc->akgh/dot_general | solution.py:58
  174.4 0.0 all-reduce.3.cloned.1.call-update
  174.4 157.0 %all-reduce.3.cloned.1.call-done = f32[128,4,64,64]{0,3,2,1:T(8,128)} async-done(((f32[128,4,64,64]{0,3,2,1:T(8,128)}), f32[128,4,64,64]{0,3,2,1:T(8,128)}) %all-reduce.3.cloned.1.call-update) | async-done | bytes 8388624 | tf_op jit(solution)/shard_map/psum | solution.py:66
  331.4 6.8 %multiply_convert_fusion = bf16[128,4,64,64]{0,3,2,1:T(8,128)(2,1)} fusion(f32[128,4,64,64]{0,3,2,1:T(8,128)} %all-reduce.3.cloned.1.call-done, f32[4,64,64]{2,1,0:T(8,128)S(1)} %pad_convert_fusion), kind=kLoop, calls=%fused_computation.16 | loop fusion | flops 8388608 | bytes 12648448 | tf_op jit(solution)/shard_map/convert_element_type | solution.py:67
  338.2 12.9 %copy.30 = bf16[128,4,64,64]{3,2,1,0:T(8,128)(2,1)} copy(bf16[128,4,64,64]{0,3,2,1:T(8,128)(2,1)} %multiply_convert_fusion) | data formatting | bytes 8388608 | tf_op jit(solution)/shard_map/convert_element_type | solution.py:67
  351.2 13.1 %fusion.7 = bf16[128,64,256]{2,1,0:T(8,128)(2,1)} fusion(bf16[128,4,64,64]{3,2,1,0:T(8,128)(2,1)} %copy.30, bf16[128,3,64,256]{3,2,1,0:T(8,128)(2,1)} %bitcast.54, bf16[128,1,64,256]{3,2,1,0:T(8,128)(2,1)} %bitcast.6, bf16[64,128,256]{2,0,1:T(8,128)(2,1)} %all-to-all-done), kind=kOutput, calls=%fused_computation.14 | convolution fusion | flops 1088421888 | bytes 29360128 | tf_op jit(solution)/shard_map/akgh,akhc->agc/dot_general | solution.py:68
  364.3 60.1 %all_to_all.32 = bf16[128,64,256]{2,1,0:T(8,128)(2,1)S(1)} all-to-all(bf16[128,64,256]{2,1,0:T(8,128)(2,1)} %fusion.7), channel_id=1, replica_groups=mesh['grid'=32,'rep'=4] {'grid','rep'}, dimensions={0} | all-to-all | bytes 8388608 | tf_op jit(solution)/shard_map/all_to_all | solution.py:71
  424.3 2.3 copy.37
  (9 shorter events, 0.1 us)
Async XLA Ops:
  50.2 4.8 %copy-start.1 = (f32[2048,1024]{1,0:T(8,128)S(1)}, f32[2048,1024]{1,0:T(8,128)}, u32[]{:S(2)}) copy-start(f32[2048,1024]{1,0:T(8,128)} %copy.24) | copy-start | bytes 25165828
  56.3 5.1 %copy-start.4 = (f32[64]{0:T(128)S(1)}, f32[64]{0:T(128)}, u32[]{:S(2)}) copy-start(f32[64]{0:T(128)} %param.10) | copy-start | bytes 772
  56.3 5.1 %copy-start.5 = (s32[64]{0:T(128)S(1)}, s32[64]{0:T(128)}, u32[]{:S(2)}) copy-start(s32[64]{0:T(128)} %param.11) | copy-start | bytes 772
  56.3 5.1 %copy-start.6 = (s32[64]{0:T(128)S(1)}, s32[64]{0:T(128)}, u32[]{:S(2)}) copy-start(s32[64]{0:T(128)} %param.12) | copy-start | bytes 772
  56.3 5.1 %copy-start = (bf16[64,32768]{1,0:T(8,128)(2,1)S(1)}, bf16[64,32768]{1,0:T(8,128)(2,1)}, u32[]{:S(2)}) copy-start(bf16[64,32768]{1,0:T(8,128)(2,1)} %param.7) | copy-start | bytes 12582916
  56.4 5.1 %copy-start.2 = (f32[32768]{0:T(1024)S(1)}, f32[32768]{0:T(1024)}, u32[]{:S(2)}) copy-start(f32[32768]{0:T(1024)} %param.9) | copy-start | bytes 393220
  65.0 14.8 %copy-start.3 = (s32[128,3]{0,1:T(4,128)S(1)}, s32[128,3]{0,1:T(4,128)}, u32[]{:S(2)}) copy-start(s32[128,3]{0,1:T(4,128)} %param.13) | copy-start | bytes 4612
  67.6 64.8 %all-to-all-start = ((bf16[64,128,256]{2,0,1:T(8,128)(2,1)}), bf16[64,128,256]{2,0,1:T(8,128)(2,1)}, u32[]{:S(2)}, u32[]{:S(2)}) async-start(bf16[64,128,256]{2,0,1:T(8,128)(2,1)} %bitcast.50), calls=%async_computation | async-start | bytes 8388608 | tf_op jit(solution)/shard_map/all_to_all | solution.py:53
  79.6 251.8 %all-reduce.3.cloned.1.call-start = ((), (), s32[]{:S(2)}) async-start(), calls=%async_computation.2 | async-start | bytes 16777216 | tf_op jit(solution)/shard_map/psum | solution.py:66
Sparse Core Ops, SparseCore 0:
  174.5 156.8 all-reduce.2
where the time goes:
time: 435 us; the launch traced here: 433 us
  waiting for transfers between devices  209 us (48%)
  local copies, waits for them, and re-layouts  85.2 us (20%)
  blocking collectives  60.1 us (14%)
  matrix products  36.1 us (8%)
  other arithmetic  17.1 us (4%)
  between operations  13.6 us (3%)
  starting transfers between devices  12.2 us (3%)
    psum x1, waiting for transfers between devices, on_device(): summed = lax.psum(local_intersection, ('grid', 'rep'))  157 us
    all_to_all x1, blocking collectives, on_device(): lax.all_to_all(result_grid, ('grid', 'rep'), split_axis=0, concat_axis=1,...  60.1 us
    all_to_all x1, waiting for transfers between devices, on_device(): lax.all_to_all(refined, ('grid', 'rep'), split_axis=1, concat_axis=0, til...  52.2 us
    dot_general x1, local copies, waits for them, and re-layouts, on_device(): jnp.einsum('agc,akhc->akgh', grouped, stacked, preferred_element_type=jnp...  15.7 us
    gather x1, local copies, waits for them, and re-layouts, on_device(): partner_rows = grouped[partner_groups]  13.5 us
    dot_general x1, matrix products, on_device(): jnp.einsum('akgh,akhc->agc', coupling, stacked, preferred_element_type=jn...  13.1 us
    convert_element_type x1, local copies, waits for them, and re-layouts, on_device(): (0.5 * (summed * weight - identity_block[None])).astype(jnp.bfloat16)  12.9 us
    dot_general x1, matrix products, on_device(): jnp.einsum('agc,akhc->akgh', grouped, stacked, preferred_element_type=jnp...  12.7 us
  transfers between devices with their start and end apart: 2, of which 2 were waited for; matrix products, arithmetic and copies ran while one was open for 0% of the time, Pallas kernels for 0%

commit v1 on v0

--- a/solution.py
+++ b/solution.py
@@ -63,7 +63,8 @@
         [jnp.eye(GROUP, dtype=jnp.float32)[None], jnp.zeros((PARTNERS, GROUP, GROUP), jnp.float32)],
         axis=0,
     )
-    summed = lax.psum(local_intersection, ("grid", "rep"))
+    inner = lax.psum(local_intersection, "rep")
+    summed = lax.psum(inner, "grid")
     coupling = (0.5 * (summed * weight - identity_block[None])).astype(jnp.bfloat16)
     shifted = jnp.einsum("akgh,akhc->agc", coupling, stacked, preferred_element_type=jnp.float32)
     result_grid = (grouped.astype(jnp.float32) - shifted).astype(jnp.bfloat16)

time: 435 us -> 558 us (1.28)
  waiting for transfers between devices: 209 us -> 332 us
    psum x1 -> x2, waiting for transfers between devices: 157 us -> 279 us  [the longest x1 156 us: on_device(): inner = lax.psum(local_intersection, 'rep')]
  transfers between devices with their start and end apart: 2 -> 3, of which waited for: 2 -> 3; matrix products, arithmetic and copies ran while one was open for 0% -> 0% of each run, Pallas kernels for 0% -> 0%
where the time goes in v1:
time: 558 us; the launch traced here: 557 us
  waiting for transfers between devices  332 us (59%)
  local copies, waits for them, and re-layouts  85.2 us (15%)
  blocking collectives  61.1 us (11%)
  matrix products  36.1 us (6%)
  other arithmetic  17.1 us (3%)
  between operations  13.6 us (2%)
  starting transfers between devices  12.2 us (2%)
    psum x1, waiting for transfers between devices, on_device(): inner = lax.psum(local_intersection, 'rep')  156 us
    psum x1, waiting for transfers between devices, on_device(): summed = lax.psum(inner, 'grid')  124 us
    all_to_all x1, blocking collectives, on_device(): lax.all_to_all(result_grid, ('grid', 'rep'), split_axis=0, concat_axis=1,...  61.1 us
    all_to_all x1, waiting for transfers between devices, on_device(): lax.all_to_all(refined, ('grid', 'rep'), split_axis=1, concat_axis=0, til...  52.2 us
    dot_general x1, local copies, waits for them, and re-layouts, on_device(): jnp.einsum('agc,akhc->akgh', grouped, stacked, preferred_element_type=jnp...  15.7 us
    gather x1, local copies, waits for them, and re-layouts, on_device(): partner_rows = grouped[partner_groups]  13.5 us
    dot_general x1, matrix products, on_device(): jnp.einsum('akgh,akhc->agc', coupling, stacked, preferred_element_type=jn...  13.1 us
    convert_element_type x1, local copies, waits for them, and re-layouts, on_device(): (0.5 * (summed * weight - identity_block[None])).astype(jnp.bfloat16)  12.9 us
  transfers between devices with their start and end apart: 3, of which 3 were waited for; matrix products, arithmetic and copies ran while one was open for 0% of the time, Pallas kernels for 0%

profile of v1, /device:TPU:1, one launch (start us, length us, event | category | flops | bytes accessed | tf_op | source)
XLA Modules:
  0.0 556.9 jit_solution(17999985867652524109)
XLA Ops:
  6.6 0.7 convert_element_type.56
  7.2 0.1 select_reduce_fusion
  7.4 5.9 %add_convert_fusion = bf16[32,32,32,32]{3,2,1,0:T(8,128)(2,1)} fusion(f32[32,32]{1,0:T(8,128)S(1)} %select_reduce_fusion, f32[32,32]{1,0:T(8,128)S(1)} %fusion.13), kind=kLoop, calls=%fused_computation.2 | loop fusion | flops 4194304 | bytes 2105344 | tf_op jit(solution)/shard_map/convert_element_type | solution.py:35
  13.3 11.3 %convert_element_type.59 = bf16[1024,1024]{1,0:T(8,128)(2,1)S(1)} reshape(bf16[32,32,32,32]{3,2,1,0:T(8,128)(2,1)} %add_convert_fusion) | data formatting | bytes 4194304 | tf_op jit(solution)/shard_map/convert_element_type | solution.py:35
  24.6 7.4 %reshape.111 = bf16[2048,1024]{1,0:T(8,128)(2,1)} reshape(bf16[64,32768]{1,0:T(8,128)(2,1)} %param.7) | data formatting | bytes 8388608 | tf_op jit(solution)/shard_map/reshape | solution.py:39
  32.0 9.0 %convolution_bitcast_fusion = f32[2048,1024]{0,1:T(8,128)} fusion(bf16[1024,1024]{1,0:T(8,128)(2,1)S(1)} %convert_element_type.59, bf16[2048,1024]{1,0:T(8,128)(2,1)} %reshape.111), kind=kOutput, calls=%fused_computation.18 | convolution fusion | flops 4294967296 | bytes 14680064 | tf_op jit(solution)/shard_map/dot_general | solution.py:38
  41.0 9.2 %copy.24 = f32[2048,1024]{1,0:T(8,128)} copy(f32[2048,1024]{0,1:T(8,128)} %convolution_bitcast_fusion) | data formatting | bytes 16777216 | tf_op jit(solution)/shard_map/dot_general | solution.py:38
  50.2 0.0 copy-start.1
  50.2 4.8 copy.38
  55.0 0.0 copy-done.1
  55.0 1.3 bitcast_add_fusion
  56.3 0.0 copy-start.4
  56.3 0.0 copy-start.5
  56.3 0.0 copy-start.6
  56.3 0.0 copy-start
  56.4 0.0 copy-start.2
  56.4 5.0 copy.39
  61.4 0.0 copy-done.4
  61.4 0.0 copy-done.5
  61.5 0.0 copy-done.6
  61.5 0.0 copy-done
  61.5 0.0 copy-done.2
  61.5 3.5 fusion.8
  65.0 0.0 copy-start.3
  65.1 2.6 copy.41
  67.6 11.9 %all-to-all-start = ((bf16[64,128,256]{2,0,1:T(8,128)(2,1)}), bf16[64,128,256]{2,0,1:T(8,128)(2,1)}, u32[]{:S(2)}, u32[]{:S(2)}) async-start(bf16[64,128,256]{2,0,1:T(8,128)(2,1)} %bitcast.50), calls=%async_computation | async-start | bytes 8388608 | tf_op jit(solution)/shard_map/all_to_all | solution.py:53
  79.6 0.3 all-reduce.4.cloned.1.call-start
  79.9 0.0 copy-done.3
  79.9 0.1 copy.27
  80.0 0.2 reshape.117
  80.2 52.2 %all-to-all-done = bf16[64,128,256]{2,0,1:T(8,128)(2,1)} async-done(((bf16[64,128,256]{2,0,1:T(8,128)(2,1)}), bf16[64,128,256]{2,0,1:T(8,128)(2,1)}, u32[]{:S(2)}, u32[]{:S(2)}) %all-to-all-start) | async-done | bytes 4194336 | tf_op jit(solution)/shard_map/all_to_all | solution.py:53
  132.4 13.5 %gather_fusion = bf16[384,64,256]{2,1,0:T(8,128)(2,1)} fusion(bf16[128,64,256]{2,1,0:T(8,128)(2,1)} %bitcast.4, s32[1024]{0:T(1024)S(1)} %pad_clamp_fusion), kind=kCustom, calls=%fused_computation | custom fusion | bytes 25167360 | tf_op jit(solution)/shard_map/gather | solution.py:56
  145.9 12.7 %fusion.1 = f32[128,4,64,64]{3,2,1,0:T(8,128)} fusion(bf16[128,3,64,256]{3,2,1,0:T(8,128)(2,1)} %bitcast.53, bf16[128,1,64,256]{3,2,1,0:T(8,128)(2,1)} %bitcast.6, bf16[64,128,256]{2,0,1:T(8,128)(2,1)} %all-to-all-done), kind=kOutput, calls=%fused_computation.7 | convolution fusion | flops 1082130432 | bytes 29360128 | tf_op jit(solution)/shard_map/agc,akhc->akgh/dot_general | solution.py:58
  158.6 15.7 %copy.29 = f32[128,4,64,64]{0,2,3,1:T(8,128)} copy(f32[128,4,64,64]{3,2,1,0:T(8,128)} %fusion.1) | data formatting | bytes 16777216 | tf_op jit(solution)/shard_map/agc,akhc->akgh/dot_general | solution.py:58
  174.4 0.0 all-reduce.4.cloned.1.call-update
  174.4 0.0 all-reduce.6.cloned.1.call-start
  174.4 155.7 %all-reduce.4.cloned.1.call-done = f32[128,4,64,64]{0,3,2,1:T(8,128)} async-done(((f32[128,4,64,64]{0,3,2,1:T(8,128)}), f32[128,4,64,64]{0,3,2,1:T(8,128)}) %all-reduce.4.cloned.1.call-update) | async-done | bytes 8388624 | tf_op jit(solution)/shard_map/psum | solution.py:66
  330.2 0.0 all-reduce.6.cloned.1.call-update
  330.3 123.5 %all-reduce.6.cloned.1.call-done = f32[128,4,64,64]{0,3,2,1:T(8,128)} async-done(((f32[128,4,64,64]{0,3,2,1:T(8,128)}), f32[128,4,64,64]{0,3,2,1:T(8,128)}) %all-reduce.6.cloned.1.call-update) | async-done | bytes 8388624 | tf_op jit(solution)/shard_map/psum | solution.py:67
  453.8 6.8 %multiply_convert_fusion = bf16[128,4,64,64]{0,3,2,1:T(8,128)(2,1)} fusion(f32[128,4,64,64]{0,3,2,1:T(8,128)} %all-reduce.6.cloned.1.call-done, f32[4,64,64]{2,1,0:T(8,128)S(1)} %pad_convert_fusion), kind=kLoop, calls=%fused_computation.16 | loop fusion | flops 8388608 | bytes 12648448 | tf_op jit(solution)/shard_map/convert_element_type | solution.py:68
  460.6 12.9 %copy.30 = bf16[128,4,64,64]{3,2,1,0:T(8,128)(2,1)} copy(bf16[128,4,64,64]{0,3,2,1:T(8,128)(2,1)} %multiply_convert_fusion) | data formatting | bytes 8388608 | tf_op jit(solution)/shard_map/convert_element_type | solution.py:68
  473.6 13.1 %fusion.7 = bf16[128,64,256]{2,1,0:T(8,128)(2,1)} fusion(bf16[128,4,64,64]{3,2,1,0:T(8,128)(2,1)} %copy.30, bf16[128,3,64,256]{3,2,1,0:T(8,128)(2,1)} %bitcast.54, bf16[128,1,64,256]{3,2,1,0:T(8,128)(2,1)} %bitcast.6, bf16[64,128,256]{2,0,1:T(8,128)(2,1)} %all-to-all-done), kind=kOutput, calls=%fused_computation.14 | convolution fusion | flops 1088421888 | bytes 29360128 | tf_op jit(solution)/shard_map/akgh,akhc->agc/dot_general | solution.py:69
  486.6 61.1 %all_to_all.32 = bf16[128,64,256]{2,1,0:T(8,128)(2,1)S(1)} all-to-all(bf16[128,64,256]{2,1,0:T(8,128)(2,1)} %fusion.7), channel_id=1, replica_groups=mesh['grid'=32,'rep'=4] {'grid','rep'}, dimensions={0} | all-to-all | bytes 8388608 | tf_op jit(solution)/shard_map/all_to_all | solution.py:72
  547.8 2.3 copy.37
  (9 shorter events, 0.1 us)
Async XLA Ops:
  50.2 4.8 copy-start.1
  56.3 5.1 copy-start.4
  56.3 5.1 copy-start.5
  56.3 5.1 copy-start.6
  56.3 5.1 copy-start
  56.4 5.1 copy-start.2
  65.0 14.8 %copy-start.3 = (s32[128,3]{0,1:T(4,128)S(1)}, s32[128,3]{0,1:T(4,128)}, u32[]{:S(2)}) copy-start(s32[128,3]{0,1:T(4,128)} %param.13) | copy-start | bytes 4612
  67.6 64.8 %all-to-all-start = ((bf16[64,128,256]{2,0,1:T(8,128)(2,1)}), bf16[64,128,256]{2,0,1:T(8,128)(2,1)}, u32[]{:S(2)}, u32[]{:S(2)}) async-start(bf16[64,128,256]{2,0,1:T(8,128)(2,1)} %bitcast.50), calls=%async_computation | async-start | bytes 8388608 | tf_op jit(solution)/shard_map/all_to_all | solution.py:53
  79.6 250.6 %all-reduce.4.cloned.1.call-start = ((), (), s32[]{:S(2)}) async-start(), calls=%async_computation.2 | async-start | bytes 16777216 | tf_op jit(solution)/shard_map/psum | solution.py:66
  174.4 279.4 %all-reduce.6.cloned.1.call-start = ((), (), s32[]{:S(2)}) async-start(), calls=%async_computation.3 | async-start | bytes 16777216 | tf_op jit(solution)/shard_map/psum | solution.py:67
Sparse Core Ops, SparseCore 0:
  174.5 155.6 all-reduce.3
  333.6 120.1 all-reduce.5
